TPU v7x, 256 devices: a whole 4x4x8 slice. The times are simulated.
256 devices in a mesh: rows: 32 (over z, x), cols: 8 (over y, core).
Axes of the slice: x: 4, y: 4, z: 8, core: 2. Of those that a mesh axis runs over, the one named last changes fastest.
Arguments:
- features: bfloat16 [524288, 440], P(('rows', 'cols')), may hold values from -12 to 12
- residual: float32 [524288, 147], P(('rows', 'cols')), may hold values from -6 to 6
- coeffs: float32 [524288, 147], P(('rows', 'cols')), may hold values from -3 to 3
- block_inverse: float32 [2, 2048, 2048], P(None, ('rows', 'cols')), may hold values from -0.0234375 to 0.0234375
- block_index: int32 [2, 2048], P(None, 'cols'), may hold values from 0 to 2047, as said below
- owners: int32 [2], replicated, may hold values from 0 to 31
Outputs:
- new_coeffs: float32 [524288, 147], P(('rows', 'cols'))
- new_residual: float32 [524288, 147], P(('rows', 'cols'))
Inputs may be any that keep to these rules, and one draw needn't show every extreme that they name: `block_index`: for each step and each aligned run of 256 positions, the indices are distinct.
All inputs are finite; a program needn't handle non-finite values.
Results may differ from a plain program's by a relative error of at most 0.0028.
Values may be sent and summed in bfloat16 or wider, within the bound.
A program may use at most 64 MiB of HBM per device.

v0:
```python
import jax
import jax.numpy as jnp
from jax import lax
from jax.sharding import Mesh
from jax.sharding import PartitionSpec as P

ROWS = ("rows_0", "rows_1")
COLS = ("cols_0", "cols_1")
ROWS_COLS = ("rows_0", "rows_1", "cols_0", "cols_1")
penalty = 0.5


def from_root(value, axes, root):
    value = jnp.where(lax.axis_index(axes) == root, value, jnp.zeros_like(value))
    for axis in axes:
        value = lax.psum(value, axis)
    return value


def in_order(parts, dim):
    shape = list(parts.shape[1:])
    shape[dim] *= parts.shape[0]
    return jnp.moveaxis(parts, 0, dim).reshape(shape)


def copy_for_each(value, axis):
    copies = jnp.broadcast_to(value, (lax.axis_size(axis), *value.shape))
    return lax.all_to_all(copies, axis, split_axis=0, concat_axis=0, tiled=True)


def collect(value, axis, dim):
    return in_order(copy_for_each(value, axis), dim)


def from_root_2(value, axis, root):
    return lax.dynamic_index_in_dim(lax.all_gather(value, axis), root, 0, keepdims=False)


def stacked_from(value, axes, order):
    parts = value[None]
    for k in order:
        parts = lax.all_gather(parts, axes[k], axis=0, tiled=True)
    block = [lax.axis_size(axes[k]) for k in reversed(order)]
    parts = parts.reshape(*block, *value.shape)
    turned = sorted(range(len(order)), key=lambda place: order[len(order) - 1 - place])
    return parts.transpose(*turned, *range(len(order), parts.ndim)).reshape(-1, *value.shape)


def gather_axes(value, axes, order, dim):
    return in_order(stacked_from(value, axes, order), dim)


def per_device(features, residual, coeffs, block_inverse, block_index, owners):
    frame_count = features.shape[0]
    feature_width = features.shape[1]
    per_col = block_index.shape[1]
    row_block = min(512, frame_count)
    exponent = -1.0 / feature_width
    my_row = lax.axis_index(ROWS)
    my_col = lax.axis_index(COLS)
    squares = jnp.sum(jnp.square(features.astype(jnp.float32)), axis=1)
    feature_blocks = features.reshape(frame_count // row_block, row_block, feature_width)
    norm_blocks = squares.reshape(frame_count // row_block, row_block)
    for step_id in range(block_index.shape[0]):
        chosen_rows = block_index[step_id]
        owner_row = owners[step_id]
        mine_feat = jnp.take(features, chosen_rows, axis=0)
        mine_res = jnp.take(residual, chosen_rows, axis=0)
        row_piece = from_root(mine_feat, ROWS, owner_row)
        chosen = collect(row_piece, COLS, 0)
        res_piece = from_root_2(mine_res, ROWS, owner_row)
        picked_res = collect(res_piece, COLS, 0)
        my_update = jnp.dot(
            block_inverse[step_id],
            picked_res,
            precision=lax.Precision.HIGHEST,
            preferred_element_type=jnp.float32,
        ).astype(jnp.bfloat16)
        update = gather_axes(my_update, ROWS_COLS, (1, 0, 2, 3), 0)
        chosen_norms = jnp.sum(jnp.square(chosen.astype(jnp.float32)), axis=1)

        def kernel_rows(operands):
            block_rows, block_norms = operands
            inner = lax.dot_general(
                block_rows, chosen, (((1,), (1,)), ((), ())), preferred_element_type=jnp.float32
            )
            distance = block_norms[:, None] + chosen_norms[None, :] - 2.0 * inner
            kernel = jnp.exp(distance * exponent).astype(jnp.bfloat16)
            return jnp.dot(kernel, update, preferred_element_type=jnp.float32)

        change = lax.map(kernel_rows, (feature_blocks, norm_blocks)).reshape(frame_count, -1)
        residual = residual - change
        is_owner = jnp.where(my_row == owner_row, 1.0, 0.0).astype(jnp.float32)
        mine_update = (
            lax.dynamic_slice_in_dim(update, my_col * per_col, per_col, 0).astype(jnp.float32)
            * is_owner
        )
        residual = residual.at[chosen_rows].add(-penalty * mine_update)
        coeffs = coeffs.at[chosen_rows].add(mine_update)
    return (coeffs, residual)


def solution(mesh):
    split = Mesh(mesh.devices.reshape(8, 4, 4, 2), ("rows_0", "rows_1", "cols_0", "cols_1"))
    in_specs = (
        P(ROWS_COLS, None),
        P(ROWS_COLS, None),
        P(ROWS_COLS, None),
        P(None, ROWS_COLS, None),
        P(None, COLS),
        P(),
    )
    out_specs = (P(ROWS_COLS, None), P(ROWS_COLS, None))
    return jax.shard_map(
        per_device, mesh=split, in_specs=in_specs, out_specs=out_specs, check_vma=False
    )
```

profile of v0, /device:TPU:1, one launch (start us, length us, event | category | flops | bytes accessed | tf_op | source)
XLA Modules:
  0.0 525.2 jit_solution(5898855721030536369)
XLA Ops:
  21.6 72.7 %all-reduce.5.cloned.1.call-done = (bf16[256,440]{1,0:T(8,128)(2,1)}, bf16[256,440]{1,0:T(8,128)(2,1)}) async-done(((bf16[256,440]{1,0:T(8,128)(2,1)}, bf16[256,440]{1,0:T(8,128)(2,1)}), (bf16[256,440]{1,0:T(8,128)(2,1)}, bf16[256,440]{1,0:T(8,128)(2,1)})) %all-reduce.5.cloned.1.call-update) | async-done | bytes 450576 | tf_op jit(solution)/shard_map/psum | solution.py:16
  97.1 49.7 %all-reduce.7.cloned.1.call-done = (bf16[256,440]{1,0:T(8,128)(2,1)}, bf16[256,440]{1,0:T(8,128)(2,1)}) async-done(((bf16[256,440]{1,0:T(8,128)(2,1)}, bf16[256,440]{1,0:T(8,128)(2,1)}), (bf16[256,440]{1,0:T(8,128)(2,1)}, bf16[256,440]{1,0:T(8,128)(2,1)})) %all-reduce.7.cloned.1.call-update) | async-done | bytes 450576 | tf_op jit(solution)/shard_map/psum | solution.py:16
  149.2 7.2 %all-to-all-start.1 = ((bf16[8,256,440]{1,2,0:T(8,128)(2,1)}), bf16[8,256,440]{1,2,0:T(8,128)(2,1)S(1)}, u32[]{:S(2)}, u32[]{:S(2)}) async-start(bf16[8,256,440]{1,2,0:T(8,128)(2,1)} %broadcast_in_dim.53), calls=%async_computation.1 | async-start | bytes 3604480 | tf_op jit(solution)/shard_map/all_to_all | solution.py:28
  158.1 40.6 %all-gather.7.cloned.1.call-done = f32[8192,147]{1,0:T(8,128)} async-done(((f32[256,147]{1,0:T(8,128)}), f32[8192,147]{1,0:T(8,128)}) %all-gather.7.cloned.1.call-update) | async-done | bytes 4816912 | tf_op jit(solution)/shard_map/all_gather | solution.py:36
  200.9 5.9 %all-to-all-start = ((f32[8,256,147]{1,2,0:T(8,128)}), f32[8,256,147]{1,2,0:T(8,128)S(1)}, u32[]{:S(2)}, u32[]{:S(2)}) async-start(f32[8,256,147]{1,2,0:T(8,128)} %broadcast_in_dim.51), calls=%async_computation | async-start | bytes 2490368 | tf_op jit(solution)/shard_map/all_to_all | solution.py:28
  211.8 12.0 %all-to-all-done = f32[8,256,147]{1,2,0:T(8,128)S(1)} async-done(((f32[8,256,147]{1,2,0:T(8,128)}), f32[8,256,147]{1,2,0:T(8,128)S(1)}, u32[]{:S(2)}, u32[]{:S(2)}) %all-to-all-start) | async-done | bytes 1204256 | tf_op jit(solution)/shard_map/all_to_all | solution.py:28
  226.2 9.1 %all-gather.1 = bf16[32,147]{1,0:T(8,128)(2,1)S(1)} all-gather(bf16[8,147]{1,0:T(8,128)(2,1)S(1)} %fusion.18), channel_id=3, replica_groups=mesh['rows_0'=8,'rows_1'=4,'cols_0'=4,'cols_1'=2] {'rows_1'}, dimensions={0}, use_global_device_ids=true | all-gather | bytes 11760 | tf_op jit(solution)/shard_map/all_gather | solution.py:42
  235.3 18.3 %all_gather.39 = bf16[32,8,147]{2,1,0:T(8,128)(2,1)S(1)} all-gather(bf16[4,8,147]{2,1,0:T(8,128)(2,1)S(1)} %bitcast.119), channel_id=1, replica_groups=mesh['rows_0'=8,'rows_1'=4,'cols_0'=4,'cols_1'=2] {'rows_0'}, dimensions={0}, use_global_device_ids=true | all-gather | bytes 84672 | tf_op jit(solution)/shard_map/all_gather | solution.py:42
  253.6 9.9 %all_gather.40 = bf16[128,8,147]{2,1,0:T(8,128)(2,1)S(1)} all-gather(bf16[32,8,147]{2,1,0:T(8,128)(2,1)S(1)} %all_gather.39), channel_id=1, replica_groups=mesh['rows_0'=8,'rows_1'=4,'cols_0'=4,'cols_1'=2] {'cols_0'}, dimensions={0}, use_global_device_ids=true | all-gather | bytes 376320 | tf_op jit(solution)/shard_map/all_gather | solution.py:42
  264.0 14.9 %all_gather.41 = bf16[256,8,147]{0,1,2:T(8,128)(2,1)S(1)} all-gather(bf16[128,8,147]{0,1,2:T(8,128)(2,1)S(1)} %copy.49), channel_id=1, replica_groups=mesh['rows_0'=8,'rows_1'=4,'cols_0'=4,'cols_1'=2] {'cols_1'}, dimensions={0}, use_global_device_ids=true | all-gather | bytes 903168 | tf_op jit(solution)/shard_map/all_gather | solution.py:42
  281.9 14.0 %while.20 = (s32[]{:T(128)}, f32[4,512,147]{1,2,0:T(8,128)S(1)}, f32[4,512]{1,0:T(4,128)S(1)}, f32[2048]{0:T(1024)S(1)}, bf16[4,512,440]{2,1,0:T(8,128)(2,1)}, /...) while((s32[]{:T(128)}, f32[4,512,147]{1,2,0:T(8,128)S(1)}, f32[4,512]{1,0:T(4,128)S(1)}, ...), condition=%wide.region_6.9_spmd, body=%wide.region_5.8_spmd.sunk | while | flops 1236271104 | bytes 3996769 | solution.py:91
  306.9 4.6 all-to-all-start.3
  313.6 84.1 %all-gather.9.cloned.1.call-done = f32[8192,147]{1,0:T(8,128)} async-done(((f32[256,147]{1,0:T(8,128)}), f32[8192,147]{1,0:T(8,128)}) %all-gather.9.cloned.1.call-update) | async-done | bytes 4816912 | tf_op jit(solution)/shard_map/all_gather | solution.py:36
  399.9 5.8 %all-to-all-start.2 = ((f32[8,256,147]{1,2,0:T(8,128)}), f32[8,256,147]{1,2,0:T(8,128)S(1)}, u32[]{:S(2)}, u32[]{:S(2)}) async-start(f32[8,256,147]{1,2,0:T(8,128)} %broadcast_in_dim.54), calls=%async_computation.2 | async-start | bytes 2490368 | tf_op jit(solution)/shard_map/all_to_all | solution.py:28
  414.1 5.1 scatter_custom_fusion
  424.7 9.1 %all-gather.3 = bf16[32,147]{1,0:T(8,128)(2,1)S(1)} all-gather(bf16[8,147]{1,0:T(8,128)(2,1)S(1)} %fusion.19), channel_id=5, replica_groups=mesh['rows_0'=8,'rows_1'=4,'cols_0'=4,'cols_1'=2] {'rows_1'}, dimensions={0}, use_global_device_ids=true | all-gather | bytes 11760 | tf_op jit(solution)/shard_map/all_gather | solution.py:42
  433.8 18.3 %all_gather.45 = bf16[32,8,147]{2,1,0:T(8,128)(2,1)S(1)} all-gather(bf16[4,8,147]{2,1,0:T(8,128)(2,1)S(1)} %bitcast.120), channel_id=1, replica_groups=mesh['rows_0'=8,'rows_1'=4,'cols_0'=4,'cols_1'=2] {'rows_0'}, dimensions={0}, use_global_device_ids=true | all-gather | bytes 84672 | tf_op jit(solution)/shard_map/all_gather | solution.py:42
  452.1 9.9 %all_gather.46 = bf16[128,8,147]{2,1,0:T(8,128)(2,1)S(1)} all-gather(bf16[32,8,147]{2,1,0:T(8,128)(2,1)S(1)} %all_gather.45), channel_id=1, replica_groups=mesh['rows_0'=8,'rows_1'=4,'cols_0'=4,'cols_1'=2] {'cols_0'}, dimensions={0}, use_global_device_ids=true | all-gather | bytes 376320 | tf_op jit(solution)/shard_map/all_gather | solution.py:42
  462.5 15.1 %all_gather.47 = bf16[256,8,147]{0,1,2:T(8,128)(2,1)} all-gather(bf16[128,8,147]{0,1,2:T(8,128)(2,1)S(1)} %copy.62), channel_id=1, replica_groups=mesh['rows_0'=8,'rows_1'=4,'cols_0'=4,'cols_1'=2] {'cols_1'}, dimensions={0}, use_global_device_ids=true | all-gather | bytes 903168 | tf_op jit(solution)/shard_map/all_gather | solution.py:42
  480.6 5.1 scatter_custom_fusion.2
  488.4 16.6 %while.21 = (s32[]{:T(128)}, f32[4,512,147]{1,2,0:T(8,128)S(1)}, f32[4,512]{1,0:T(4,128)S(1)}, f32[2048]{0:T(1024)S(1)}, bf16[4,512,440]{2,1,0:T(8,128)(2,1)}, /...) while((s32[]{:T(128)}, f32[4,512,147]{1,2,0:T(8,128)S(1)}, f32[4,512]{1,0:T(4,128)S(1)}, ...), condition=%wide.region_13.16_spmd, body=%wide.region_12.15_spmd.sunk | while | flops 1236271104 | bytes 3996769 | solution.py:91
  492.6 4.1 fusion.63
  500.9 4.1 fusion.63
  510.0 5.1 scatter_custom_fusion.3
  (98 shorter events, 93.7 us)
Async XLA Ops:
  8.0 86.4 %all-reduce.5.cloned.1.call-start = ((), (), s32[]{:S(2)}) async-start(), calls=%async_computation.6 | async-start | bytes 1048576 | tf_op jit(solution)/shard_map/psum | solution.py:16
  14.3 3.7 copy-start.1
  16.2 78.3 %copy-start.3 = (f32[2048,147]{0,1:T(8,128)S(1)}, f32[2048,147]{0,1:T(8,128)}, u32[]{:S(2)}) copy-start(f32[2048,147]{0,1:T(8,128)} %param.15) | copy-start | bytes 3612676
  21.6 125.2 %all-reduce.7.cloned.1.call-start = ((), (), s32[]{:S(2)}) async-start(), calls=%async_computation.7 | async-start | bytes 1048576 | tf_op jit(solution)/shard_map/psum | solution.py:16
  94.4 104.3 %all-gather.7.cloned.1.call-start = ((), (), s32[]{:S(2)}) async-start(), calls=%async_computation.4 | async-start | bytes 8650752 | tf_op jit(solution)/shard_map/all_gather | solution.py:36
  95.3 53.9 %copy-start = (f32[2048,147]{1,0:T(8,128)}, f32[2048,147]{1,0:T(8,128)S(1)}, u32[]{:S(2)}) copy-start(f32[2048,147]{1,0:T(8,128)S(1)} %copy.46) | copy-start | bytes 3612676
  149.2 50.6 %all-to-all-start.1 = ((bf16[8,256,440]{1,2,0:T(8,128)(2,1)}), bf16[8,256,440]{1,2,0:T(8,128)(2,1)S(1)}, u32[]{:S(2)}, u32[]{:S(2)}) async-start(bf16[8,256,440]{1,2,0:T(8,128)(2,1)} %broadcast_in_dim.53), calls=%async_computation.1 | async-start | bytes 3604480 | tf_op jit(solution)/shard_map/all_to_all | solution.py:28
  200.9 7.8 %copy-start.6 = (s32[2,256]{1,0:T(2,128)S(1)}, s32[2,256]{1,0:T(2,128)}, u32[]{:S(2)}) copy-start(s32[2,256]{1,0:T(2,128)} %param.18) | copy-start | bytes 6148
  200.9 23.0 %all-to-all-start = ((f32[8,256,147]{1,2,0:T(8,128)}), f32[8,256,147]{1,2,0:T(8,128)S(1)}, u32[]{:S(2)}, u32[]{:S(2)}) async-start(f32[8,256,147]{1,2,0:T(8,128)} %broadcast_in_dim.51), calls=%async_computation | async-start | bytes 2490368 | tf_op jit(solution)/shard_map/all_to_all | solution.py:28
  206.8 190.9 %all-gather.9.cloned.1.call-start = ((), (), s32[]{:S(2)}) async-start(), calls=%async_computation.5 | async-start | bytes 8650752 | tf_op jit(solution)/shard_map/all_gather | solution.py:36
  224.2 0.9 copy-start.5
  280.0 2.0 copy-start.2
  303.6 1.8 copy-start.4
  306.9 91.8 %all-to-all-start.3 = ((bf16[8,256,440]{1,2,0:T(8,128)(2,1)}), bf16[8,256,440]{1,2,0:T(8,128)(2,1)}, u32[]{:S(2)}, u32[]{:S(2)}) async-start(bf16[8,256,440]{1,2,0:T(8,128)(2,1)} %broadcast_in_dim.56), calls=%async_computation.3 | async-start | bytes 3604480 | tf_op jit(solution)/shard_map/all_to_all | solution.py:28
  399.9 22.8 %all-to-all-start.2 = ((f32[8,256,147]{1,2,0:T(8,128)}), f32[8,256,147]{1,2,0:T(8,128)S(1)}, u32[]{:S(2)}, u32[]{:S(2)}) async-start(f32[8,256,147]{1,2,0:T(8,128)} %broadcast_in_dim.54), calls=%async_computation.2 | async-start | bytes 2490368 | tf_op jit(solution)/shard_map/all_to_all | solution.py:28
Sparse Core Ops, SparseCore 0:
  21.7 72.6 all-reduce.4
  96.8 49.8 all-reduce.6
Sparse Core Ops, SparseCore 1:
  98.0 100.6 all-gather.6
  305.5 92.2 all-gather.8
where the time goes:
time: 527 us; the launch traced here: 525 us
  waiting for transfers between devices  263 us (50%)
  blocking collectives  105 us (20%)
  local copies, waits for them, and re-layouts  47.4 us (9%)
  other arithmetic  33.4 us (6%)
  matrix products  32.5 us (6%)
  starting transfers between devices  23.5 us (4%)
  between operations  20.9 us (4%)
    all_gather x2, waiting for transfers between devices, from_root_2(): lax.all_gather(value, axis)  125 us
    psum x2, waiting for transfers between devices, from_root(): value = lax.psum(value, axis)  122 us
    all_gather x8, blocking collectives, stacked_from(): parts = lax.all_gather(parts, axes[k], axis=0, tiled=True)  105 us
    dot_general x8, matrix products, kernel_rows(): return jnp.dot(kernel, update, preferred_element_type=jnp.float32)  30.4 us
    all_to_all x4, starting transfers between devices, copy_for_each(): return lax.all_to_all(copies, axis, split_axis=0, concat_axis=0, tiled=True)  23.4 us
    all_to_all x4, waiting for transfers between devices, copy_for_each(): return lax.all_to_all(copies, axis, split_axis=0, concat_axis=0, tiled=True)  15.6 us
    unnamed x27, local copies, waits for them, and re-layouts  14.1 us
  transfers between devices with their start and end apart: 8, of which 6 were waited for; matrix products, arithmetic and copies ran while one was open for 5% of the time, Pallas kernels for 0%

commit v1 on v0

--- a/solution.py
+++ b/solution.py
@@ -3,11 +3,19 @@
 from jax import lax
 from jax.sharding import Mesh
 from jax.sharding import PartitionSpec as P
+from jax.lax import all_to_all, axis_size
 
 ROWS = ("rows_0", "rows_1")
 COLS = ("cols_0", "cols_1")
 ROWS_COLS = ("rows_0", "rows_1", "cols_0", "cols_1")
 penalty = 0.5
+
+
+def launch_numbers_all(a0, peer_axis):
+    return jnp.concatenate(
+        all_to_all(jnp.stack([a0 for _ in range(axis_size(peer_axis))], axis=0), peer_axis, 0, 0),
+        axis=0,
+    )
 
 
 def from_root(value, axes, root):
@@ -39,7 +47,7 @@
 def stacked_from(value, axes, order):
     parts = value[None]
     for k in order:
-        parts = lax.all_gather(parts, axes[k], axis=0, tiled=True)
+        parts = launch_numbers_all(parts, peer_axis=axes[k])
     block = [lax.axis_size(axes[k]) for k in reversed(order)]
     parts = parts.reshape(*block, *value.shape)
     turned = sorted(range(len(order)), key=lambda place: order[len(order) - 1 - place])

time: 527 us -> 589 us (1.12)
  waiting for transfers between devices: 263 us -> 361 us
  blocking collectives: 105 us -> 44 us
  starting transfers between devices: 23.5 us -> 37.4 us
  local copies, waits for them, and re-layouts: 47.4 us -> 58.7 us
    all_gather x8 -> x0, blocking collectives: 105 us -> none  [stacked_from(): parts = lax.all_gather(parts, axes[k], axis=0, tiled=True)]
    all_gather x2, waiting for transfers between devices: 125 us -> 174 us  [from_root_2(): lax.all_gather(value, axis)]
    all_to_all x0 -> x5, blocking collectives: none -> 44 us  [launch_numbers_all(): all_to_all(jnp.stack([a0 for _ in range(axis_size(peer_axis))], axis=0),...]
    all_to_all x4, waiting for transfers between devices: 15.6 us -> 57.2 us  [copy_for_each(): return lax.all_to_all(copies, axis, split_axis=0, concat_axis=0, tiled=True)]
    all_to_all x0 -> x3, starting transfers between devices: none -> 13.7 us  [launch_numbers_all(): all_to_all(jnp.stack([a0 for _ in range(axis_size(peer_axis))], axis=0),...]
    all_to_all x0 -> x3, waiting for transfers between devices: none -> 9.7 us  [launch_numbers_all(): all_to_all(jnp.stack([a0 for _ in range(axis_size(peer_axis))], axis=0),...]
    unnamed x27 -> x25, local copies, waits for them, and re-layouts: 14.1 us -> 16.9 us
  transfers between devices with their start and end apart: 8 -> 11, of which waited for: 6 -> 9; matrix products, arithmetic and copies ran while one was open for 5% -> 6% of each run, Pallas kernels for 0% -> 0%
where the time goes in v1:
time: 589 us; the launch traced here: 587 us
  waiting for transfers between devices  361 us (61%)
  local copies, waits for them, and re-layouts  58.7 us (10%)
  blocking collectives  44 us (7%)
  starting transfers between devices  37.4 us (6%)
  other arithmetic  33.1 us (6%)
  matrix products  32.5 us (6%)
  between operations  20.7 us (4%)
    all_gather x2, waiting for transfers between devices, from_root_2(): lax.all_gather(value, axis)  174 us
    psum x2, waiting for transfers between devices, from_root(): value = lax.psum(value, axis)  120 us
    all_to_all x4, waiting for transfers between devices, copy_for_each(): return lax.all_to_all(copies, axis, split_axis=0, concat_axis=0, tiled=True)  57.2 us
    all_to_all x5, blocking collectives, launch_numbers_all(): all_to_all(jnp.stack([a0 for _ in range(axis_size(peer_axis))], axis=0),...  44 us
    dot_general x8, matrix products, kernel_rows(): return jnp.dot(kernel, update, preferred_element_type=jnp.float32)  30.4 us
    all_to_all x4, starting transfers between devices, copy_for_each(): return lax.all_to_all(copies, axis, split_axis=0, concat_axis=0, tiled=True)  23.6 us
    unnamed x25, local copies, waits for them, and re-layouts  16.9 us
    all_to_all x3, starting transfers between devices, launch_numbers_all(): all_to_all(jnp.stack([a0 for _ in range(axis_size(peer_axis))], axis=0),...  13.7 us
  transfers between devices with their start and end apart: 11, of which 9 were waited for; matrix products, arithmetic and copies ran while one was open for 6% of the time, Pallas kernels for 0%

profile of v1, /device:TPU:1, one launch (start us, length us, event | category | flops | bytes accessed | tf_op | source)
XLA Modules:
  0.0 587.3 jit_solution(11105863402617033714)
XLA Ops:
  27.0 86.5 %all-gather.5.cloned.1.call-done = f32[8192,147]{1,0:T(8,128)} async-done(((f32[256,147]{1,0:T(8,128)}), f32[8192,147]{1,0:T(8,128)}) %all-gather.5.cloned.1.call-update) | async-done | bytes 4816912 | tf_op jit(solution)/shard_map/all_gather | solution.py:44
  115.7 5.7 all-to-all-start
  122.3 68.2 %all-reduce.5.cloned.1.call-done = (bf16[256,440]{1,0:T(8,128)(2,1)}, bf16[256,440]{1,0:T(8,128)(2,1)}) async-done(((bf16[256,440]{1,0:T(8,128)(2,1)}, bf16[256,440]{1,0:T(8,128)(2,1)}), (bf16[256,440]{1,0:T(8,128)(2,1)}, bf16[256,440]{1,0:T(8,128)(2,1)})) %all-reduce.5.cloned.1.call-update) | async-done | bytes 450576 | tf_op jit(solution)/shard_map/psum | solution.py:24
  190.5 51.6 %all-reduce.7.cloned.1.call-done = (bf16[256,440]{1,0:T(8,128)(2,1)}, bf16[256,440]{1,0:T(8,128)(2,1)}) async-done(((bf16[256,440]{1,0:T(8,128)(2,1)}, bf16[256,440]{1,0:T(8,128)(2,1)}), (bf16[256,440]{1,0:T(8,128)(2,1)}, bf16[256,440]{1,0:T(8,128)(2,1)})) %all-reduce.7.cloned.1.call-update) | async-done | bytes 450576 | tf_op jit(solution)/shard_map/psum | solution.py:24
  244.5 7.0 %all-to-all-start.5 = ((bf16[8,256,440]{1,2,0:T(8,128)(2,1)}), bf16[8,256,440]{1,2,0:T(8,128)(2,1)S(1)}, u32[]{:S(2)}, u32[]{:S(2)}) async-start(bf16[8,256,440]{1,2,0:T(8,128)(2,1)} %broadcast_in_dim.46), calls=%async_computation.5 | async-start | bytes 3604480 | tf_op jit(solution)/shard_map/all_to_all | solution.py:36
  254.0 20.7 %all-to-all-done.5 = bf16[8,256,440]{1,2,0:T(8,128)(2,1)S(1)} async-done(((bf16[8,256,440]{1,2,0:T(8,128)(2,1)}), bf16[8,256,440]{1,2,0:T(8,128)(2,1)S(1)}, u32[]{:S(2)}, u32[]{:S(2)}) %all-to-all-start.5) | async-done | bytes 1802272 | tf_op jit(solution)/shard_map/all_to_all | solution.py:36
  274.6 7.2 %all_to_all.60 = bf16[4,1,8,147]{3,2,1,0:T(8,128)(2,1)S(1)} all-to-all(bf16[4,1,8,147]{3,2,1,0:T(8,128)(2,1)S(1)} %stack.24), channel_id=1, replica_groups=mesh['rows_0'=8,'rows_1'=4,'cols_0'=4,'cols_1'=2] {'rows_1'}, dimensions={0} | all-to-all | bytes 18816 | tf_op jit(solution)/shard_map/all_to_all | solution.py:16
  282.5 6.7 %all-to-all-start.2 = ((bf16[8,4,8,147]{3,2,1,0:T(8,128)(2,1)}), bf16[8,4,8,147]{3,2,1,0:T(8,128)(2,1)S(1)}, u32[]{:S(2)}, u32[]{:S(2)}) async-start(bf16[8,4,8,147]{3,2,1,0:T(8,128)(2,1)} %stack.25), calls=%async_computation.2 | async-start | bytes 262144 | tf_op jit(solution)/shard_map/all_to_all | solution.py:16
  289.2 7.9 %all-to-all-done.2 = bf16[8,4,8,147]{3,2,1,0:T(8,128)(2,1)S(1)} async-done(((bf16[8,4,8,147]{3,2,1,0:T(8,128)(2,1)}), bf16[8,4,8,147]{3,2,1,0:T(8,128)(2,1)S(1)}, u32[]{:S(2)}, u32[]{:S(2)}) %all-to-all-start.2) | async-done | bytes 75296 | tf_op jit(solution)/shard_map/all_to_all | solution.py:16
  309.7 8.9 %all_to_all.61 = bf16[2,128,8,147]{1,2,3,0:T(8,128)(2,1)S(1)} all-to-all(bf16[2,128,8,147]{1,2,3,0:T(8,128)(2,1)S(1)} %copy.49), channel_id=1, replica_groups=mesh['rows_0'=8,'rows_1'=4,'cols_0'=4,'cols_1'=2] {'cols_1'}, dimensions={0} | all-to-all | bytes 1204224 | tf_op jit(solution)/shard_map/all_to_all | solution.py:16
  321.5 14.0 %while.20 = (s32[]{:T(128)}, f32[4,512,147]{1,2,0:T(8,128)S(1)}, f32[4,512]{1,0:T(4,128)S(1)}, f32[2048]{0:T(1024)S(1)}, bf16[4,512,440]{2,1,0:T(8,128)(2,1)}, /...) while((s32[]{:T(128)}, f32[4,512,147]{1,2,0:T(8,128)S(1)}, f32[4,512]{1,0:T(4,128)S(1)}, ...), condition=%wide.region_6.9_spmd, body=%wide.region_5.8_spmd.sunk | while | flops 1236271104 | bytes 3996769 | solution.py:99
  346.5 87.6 %all-gather.7.cloned.1.call-done = f32[8192,147]{1,0:T(8,128)} async-done(((f32[256,147]{1,0:T(8,128)}), f32[8192,147]{1,0:T(8,128)}) %all-gather.7.cloned.1.call-update) | async-done | bytes 4816912 | tf_op jit(solution)/shard_map/all_gather | solution.py:44
  436.3 5.7 all-to-all-start.6
  443.8 15.3 %all-to-all-done.6 = f32[8,256,147]{1,2,0:T(8,128)S(1)} async-done(((f32[8,256,147]{1,2,0:T(8,128)}), f32[8,256,147]{1,2,0:T(8,128)S(1)}, u32[]{:S(2)}, u32[]{:S(2)}) %all-to-all-start.6) | async-done | bytes 1204256 | tf_op jit(solution)/shard_map/all_to_all | solution.py:36
  461.3 5.2 all-to-all-start.11
  468.5 21.2 %all-to-all-done.11 = bf16[8,256,440]{1,2,0:T(8,128)(2,1)} async-done(((bf16[8,256,440]{1,2,0:T(8,128)(2,1)}), bf16[8,256,440]{1,2,0:T(8,128)(2,1)}, u32[]{:S(2)}, u32[]{:S(2)}) %all-to-all-start.11) | async-done | bytes 1802272 | tf_op jit(solution)/shard_map/all_to_all | solution.py:36
  489.7 6.5 %all_to_all.62 = bf16[4,1,8,147]{3,2,1,0:T(8,128)(2,1)S(1)} all-to-all(bf16[4,1,8,147]{3,2,1,0:T(8,128)(2,1)S(1)} %stack.28), channel_id=1, replica_groups=mesh['rows_0'=8,'rows_1'=4,'cols_0'=4,'cols_1'=2] {'rows_1'}, dimensions={0} | all-to-all | bytes 18816 | tf_op jit(solution)/shard_map/all_to_all | solution.py:16
  496.2 11.8 %all_to_all.63 = bf16[8,4,8,147]{3,2,1,0:T(8,128)(2,1)S(1)} all-to-all(bf16[8,4,8,147]{3,2,1,0:T(8,128)(2,1)S(1)} %stack.29), channel_id=1, replica_groups=mesh['rows_0'=8,'rows_1'=4,'cols_0'=4,'cols_1'=2] {'rows_0'}, dimensions={0} | all-to-all | bytes 150528 | tf_op jit(solution)/shard_map/all_to_all | solution.py:16
  520.9 5.1 scatter_custom_fusion
  530.0 9.6 %all_to_all.64 = bf16[2,128,8,147]{1,2,3,0:T(8,128)(2,1)} all-to-all(bf16[2,128,8,147]{1,2,3,0:T(8,128)(2,1)} %copy.62), channel_id=1, replica_groups=mesh['rows_0'=8,'rows_1'=4,'cols_0'=4,'cols_1'=2] {'cols_1'}, dimensions={0} | all-to-all | bytes 1204224 | tf_op jit(solution)/shard_map/all_to_all | solution.py:16
  542.6 5.1 scatter_custom_fusion.2
  550.5 16.6 %while.21 = (s32[]{:T(128)}, f32[4,512,147]{1,2,0:T(8,128)S(1)}, f32[4,512]{1,0:T(4,128)S(1)}, f32[2048]{0:T(1024)S(1)}, bf16[4,512,440]{2,1,0:T(8,128)(2,1)}, /...) while((s32[]{:T(128)}, f32[4,512,147]{1,2,0:T(8,128)S(1)}, f32[4,512]{1,0:T(4,128)S(1)}, ...), condition=%wide.region_13.16_spmd, body=%wide.region_12.15_spmd.sunk | while | flops 1236271104 | bytes 3996769 | solution.py:99
  554.7 4.1 fusion.63
  572.1 5.1 scatter_custom_fusion.3
  (107 shorter events, 113.9 us)
Async XLA Ops:
  8.0 105.5 %all-gather.5.cloned.1.call-start = ((), (), s32[]{:S(2)}) async-start(), calls=%async_computation.12 | async-start | bytes 8650752 | tf_op jit(solution)/shard_map/all_gather | solution.py:44
  10.6 8.8 %copy-start = (f32[2048,147]{1,0:T(8,128)}, f32[2048,147]{1,0:T(8,128)S(1)}, u32[]{:S(2)}) copy-start(f32[2048,147]{1,0:T(8,128)S(1)} %copy.46) | copy-start | bytes 3612676
  10.6 1.8 copy-start.5
  115.7 127.5 %all-to-all-start = ((f32[8,256,147]{1,2,0:T(8,128)}), f32[8,256,147]{1,2,0:T(8,128)S(1)}, u32[]{:S(2)}, u32[]{:S(2)}) async-start(f32[8,256,147]{1,2,0:T(8,128)} %broadcast_in_dim.45), calls=%async_computation | async-start | bytes 2490368 | tf_op jit(solution)/shard_map/all_to_all | solution.py:36
  121.4 69.1 %all-reduce.5.cloned.1.call-start = ((), (), s32[]{:S(2)}) async-start(), calls=%async_computation.14 | async-start | bytes 1048576 | tf_op jit(solution)/shard_map/psum | solution.py:24
  122.2 119.8 %all-reduce.7.cloned.1.call-start = ((), (), s32[]{:S(2)}) async-start(), calls=%async_computation.15 | async-start | bytes 1048576 | tf_op jit(solution)/shard_map/psum | solution.py:24
  244.5 30.1 %all-to-all-start.5 = ((bf16[8,256,440]{1,2,0:T(8,128)(2,1)}), bf16[8,256,440]{1,2,0:T(8,128)(2,1)S(1)}, u32[]{:S(2)}, u32[]{:S(2)}) async-start(bf16[8,256,440]{1,2,0:T(8,128)(2,1)} %broadcast_in_dim.46), calls=%async_computation.5 | async-start | bytes 3604480 | tf_op jit(solution)/shard_map/all_to_all | solution.py:36
  252.0 0.9 copy-start.3
  252.1 37.1 %copy-start.4 = (s32[2,256]{1,0:T(2,128)S(1)}, s32[2,256]{1,0:T(2,128)}, u32[]{:S(2)}) copy-start(s32[2,256]{1,0:T(2,128)} %param.18) | copy-start | bytes 6148
  282.5 14.7 %all-to-all-start.2 = ((bf16[8,4,8,147]{3,2,1,0:T(8,128)(2,1)}), bf16[8,4,8,147]{3,2,1,0:T(8,128)(2,1)S(1)}, u32[]{:S(2)}, u32[]{:S(2)}) async-start(bf16[8,4,8,147]{3,2,1,0:T(8,128)(2,1)} %stack.25), calls=%async_computation.2 | async-start | bytes 262144 | tf_op jit(solution)/shard_map/all_to_all | solution.py:16
  298.0 10.4 %all-to-all-start.3 = ((bf16[4,32,8,147]{3,2,1,0:T(8,128)(2,1)}), bf16[4,32,8,147]{3,2,1,0:T(8,128)(2,1)S(1)}, u32[]{:S(2)}, u32[]{:S(2)}) async-start(bf16[4,32,8,147]{3,2,1,0:T(8,128)(2,1)} %stack.26), calls=%async_computation.3 | async-start | bytes 1048576 | tf_op jit(solution)/shard_map/all_to_all | solution.py:16
  301.4 132.7 %all-gather.7.cloned.1.call-start = ((), (), s32[]{:S(2)}) async-start(), calls=%async_computation.13 | async-start | bytes 8650752 | tf_op jit(solution)/shard_map/all_gather | solution.py:44
  319.5 2.0 copy-start.2
  436.3 22.8 %all-to-all-start.6 = ((f32[8,256,147]{1,2,0:T(8,128)}), f32[8,256,147]{1,2,0:T(8,128)S(1)}, u32[]{:S(2)}, u32[]{:S(2)}) async-start(f32[8,256,147]{1,2,0:T(8,128)} %broadcast_in_dim.47), calls=%async_computation.6 | async-start | bytes 2490368 | tf_op jit(solution)/shard_map/all_to_all | solution.py:36
  461.3 28.4 %all-to-all-start.11 = ((bf16[8,256,440]{1,2,0:T(8,128)(2,1)}), bf16[8,256,440]{1,2,0:T(8,128)(2,1)}, u32[]{:S(2)}, u32[]{:S(2)}) async-start(bf16[8,256,440]{1,2,0:T(8,128)(2,1)} %broadcast_in_dim.48), calls=%async_computation.11 | async-start | bytes 3604480 | tf_op jit(solution)/shard_map/all_to_all | solution.py:36
  508.9 17.0 %all-to-all-start.9 = ((bf16[4,32,8,147]{3,2,1,0:T(8,128)(2,1)}), bf16[4,32,8,147]{3,2,1,0:T(8,128)(2,1)S(1)}, u32[]{:S(2)}, u32[]{:S(2)}) async-start(bf16[4,32,8,147]{3,2,1,0:T(8,128)(2,1)} %stack.30), calls=%async_computation.9 | async-start | bytes 1048576 | tf_op jit(solution)/shard_map/all_to_all | solution.py:16
  525.9 0.8 copy-start.1
Sparse Core Ops, SparseCore 0:
  12.6 100.8 all-gather.4
  344.9 89.1 all-gather.6
Sparse Core Ops, SparseCore 1:
  124.8 65.6 all-reduce.4
  192.7 49.3 all-reduce.6
